TPU v7x, 256 devices: a whole 4x4x8 slice. The times are simulated.
256 devices in a mesh: seq: 32 (over z_hi, x, core), tensor: 8 (over y, z_lo).
Axes of the slice: x: 4, y: 4, z: 8 (z_hi: 4, z_lo: 2; z = z_hi * 2 + z_lo), core: 2. Of those that a mesh axis runs over, the one named last changes fastest.
Arguments:
- tokens: bfloat16 [4096, 2048], P('seq'), may hold values from -6 to 6
- lengths: int32 [8], replicated, may hold values from 1 to 2048, 4096 in all
- page_table: int32 [256], replicated, may hold values from 0 to 255, each once
- attention_gain: float32 [2048], replicated, may hold values from 0.25 to 1.75
- query_weight: bfloat16 [2048, 2048], P(None, 'tensor')
- key_weight: bfloat16 [2048, 2048], P(None, 'tensor')
- value_weight: bfloat16 [2048, 2048], P(None, 'tensor'), may hold values from -0.125 to 0.125
- out_weight: bfloat16 [2048, 2048], P('tensor'), may hold values from -0.125 to 0.125
- expert_gain: float32 [2048], replicated, may hold values from 0.25 to 1.75
- router_weight: bfloat16 [2048, 64], replicated, may hold values from -0.03125 to 0.03125
- expert_ids: int32 [4096, 8], P('seq'), may hold values from 0 to 63, all different within a row; in each aligned block of 128 rows (0 to 127, 128 to 255, ...) at most 24 rows name the same one
- gate_weight: bfloat16 [64, 2048, 1024], P('seq', None, 'tensor'), may hold values from -0.125 to 0.125
- up_weight: bfloat16 [64, 2048, 1024], P('seq', None, 'tensor'), may hold values from -0.125 to 0.125
- down_weight: bfloat16 [64, 1024, 2048], P('seq', 'tensor'), may hold values from -6 to 6
Outputs:
- layer_out: bfloat16 [4096, 2048], P('seq')
- key_cache: bfloat16 [256, 16, 2048], P('seq', None, 'tensor')
- value_cache: bfloat16 [256, 16, 2048], P('seq', None, 'tensor')
Inputs may be any that keep to these rules, and one draw needn't show every extreme that they name: The 8 lengths sum to 4096; the longest is exactly 2048. `page_table`: every page number appears once. `expert_ids`: each token names 8 different experts; among the 128 tokens of one index of seq no expert is named more than 24 times, a bound that some block reaches.
All inputs are finite; a program needn't handle non-finite values.
Results may differ from a plain program's by a relative error of at most 0.023.
Values may be sent and summed in bfloat16 or wider, within the bound.
A program may use at most 128 MiB of HBM per device.

v0:
```python
import jax
import jax.numpy as jnp
from jax import lax
from jax.sharding import PartitionSpec as P

HEAD_DIM = 128
PAGE = 16
epsilon = 1e-05
rope_base = 10000.0


def rms_scale(matrix, scaling):
    mean_square = jnp.mean(matrix * matrix, axis=-1, keepdims=True)
    return matrix * lax.rsqrt(mean_square + epsilon) * scaling


def segment_info(lengths, places):
    starts = jnp.cumsum(lengths) - lengths
    inside = (places[:, None] >= starts[None, :]).astype(jnp.int32)
    segment = jnp.sum(inside, axis=1) - 1
    slot_ids = jnp.arange(starts.shape[0], dtype=jnp.int32)
    seg_start = jnp.sum(
        jnp.where(slot_ids[None, :] == segment[:, None], starts[None, :], 0), axis=1
    )
    return (segment, places - seg_start)


def rotate(matrix, position):
    half_dim = matrix.shape[-1] // 2
    frequency = jnp.exp(
        -jnp.log(rope_base) * jnp.arange(half_dim, dtype=jnp.float32) * (2.0 / matrix.shape[-1])
    )
    angles = position.astype(jnp.float32)[:, None] * frequency[None, :]
    cosine = jnp.cos(angles)[:, None, :]
    sine_part = jnp.sin(angles)[:, None, :]
    first_half = matrix[..., :half_dim]
    second = matrix[..., half_dim:]
    return jnp.concatenate(
        [first_half * cosine - second * sine_part, second * cosine + first_half * sine_part],
        axis=-1,
    )


def local(
    tokens,
    lengths,
    page_table,
    attention_gain,
    query_weight,
    key_weight,
    value_weight,
    out_weight,
    expert_gain,
    router_weight,
    expert_ids,
    gate_weight,
    up_weight,
    down_weight,
):
    row_count = tokens.shape[0]
    feature_count = tokens.shape[1]
    span_size = query_weight.shape[1]
    head_count = span_size // HEAD_DIM
    shard_id = lax.axis_index("seq")
    places = shard_id * row_count + jnp.arange(row_count, dtype=jnp.int32)
    segment, position = segment_info(lengths, places)
    stream = tokens.astype(jnp.float32)
    normed = rms_scale(stream, attention_gain).astype(jnp.bfloat16)
    queries = rotate(
        jnp.dot(normed, query_weight, preferred_element_type=jnp.float32).reshape(
            row_count, head_count, HEAD_DIM
        ),
        position,
    ).astype(jnp.bfloat16)
    key_rows = (
        rotate(
            jnp.dot(normed, key_weight, preferred_element_type=jnp.float32).reshape(
                row_count, head_count, HEAD_DIM
            ),
            position,
        )
        .astype(jnp.bfloat16)
        .reshape(row_count, span_size)
    )
    value_rows = jnp.dot(normed, value_weight, preferred_element_type=jnp.float32).astype(
        jnp.bfloat16
    )
    page_rows = row_count // PAGE
    my_pages = shard_id * page_rows + jnp.arange(page_rows, dtype=jnp.int32)
    owned = (page_table[None, :] == my_pages[:, None]).astype(jnp.bfloat16)
    score_scale = HEAD_DIM ** (-0.5)
    state = (
        jnp.full((head_count, row_count), -1e30, jnp.float32),
        jnp.zeros((head_count, row_count), jnp.float32),
        jnp.zeros((head_count, row_count, HEAD_DIM), jnp.float32),
    )
    key_piece = lax.all_gather(key_rows, "seq", axis=0, tiled=True)
    value_piece = lax.all_gather(value_rows, "seq", axis=0, tiled=True)
    piece_rows = key_piece.shape[0]
    key_pages = jnp.dot(
        owned,
        key_piece.reshape(piece_rows // PAGE, PAGE * span_size),
        preferred_element_type=jnp.float32,
    )
    value_pages = jnp.dot(
        owned,
        value_piece.reshape(piece_rows // PAGE, PAGE * span_size),
        preferred_element_type=jnp.float32,
    )
    row_peak, row_total, weighted = state
    piece_rows = key_piece.shape[0]
    key_places = jnp.arange(piece_rows, dtype=jnp.int32)
    key_segments, _ = segment_info(lengths, key_places)
    scores = (
        jnp.einsum(
            "qhd,khd->hqk",
            queries,
            key_piece.reshape(piece_rows, head_count, HEAD_DIM),
            preferred_element_type=jnp.float32,
        )
        * score_scale
    )
    allowed = (
        (segment[:, None] == key_segments[None, :]) & (key_places[None, :] <= places[:, None])
    )[None]
    new_peak = jnp.maximum(row_peak, jnp.max(jnp.where(allowed, scores, -1e30), axis=-1))
    raised = jnp.where(allowed, jnp.exp(scores - new_peak[:, :, None]), 0.0)
    row_total = jnp.sum(raised, axis=-1)
    weighted = jnp.einsum(
        "hqk,khd->hqd",
        raised.astype(jnp.bfloat16),
        value_piece.reshape(piece_rows, head_count, HEAD_DIM),
        preferred_element_type=jnp.float32,
    )
    state = (new_peak, row_total, weighted)
    state, key_pages, value_pages = (state, key_pages, value_pages)
    _, row_total, weighted = state
    attended = (
        jnp.transpose(weighted / row_total[:, :, None], (1, 0, 2))
        .reshape(row_count, span_size)
        .astype(jnp.bfloat16)
    )
    head_part = jnp.dot(attended, out_weight, preferred_element_type=jnp.float32)
    hidden = stream + lax.psum(head_part.astype(jnp.bfloat16), "tensor").astype(jnp.float32)
    moe_input = rms_scale(hidden, expert_gain).astype(jnp.bfloat16)
    expert_count = router_weight.shape[1]
    probability = jax.nn.softmax(
        jnp.dot(moe_input, router_weight, preferred_element_type=jnp.float32), axis=-1
    )
    expert_range = jnp.arange(expert_count, dtype=jnp.int32)
    chosen = jnp.sum(
        jnp.where(
            expert_ids[:, :, None] == expert_range[None, None, :], probability[:, None, :], 0.0
        ),
        axis=-1,
    )
    top_count = expert_ids.shape[1]
    flat_ids = expert_ids.reshape(-1)
    onehot = (flat_ids[:, None] == expert_range[None, :]).astype(jnp.int32)
    slot_rank = jnp.sum(jnp.cumsum(onehot, axis=0) * onehot, axis=1) - 1
    members = lax.axis_size("tensor")
    sources = lax.axis_size("seq")
    local_count = gate_weight.shape[0]
    base_room = row_count * top_count * 3 // (2 * expert_count)
    capacity = members * ((base_room + members - 1) // members)
    owners = jnp.arange(row_count * top_count, dtype=jnp.int32) // top_count
    slot_index = flat_ids * capacity + slot_rank
    row_table = (
        jnp.full((expert_count * capacity,), row_count, jnp.int32).at[slot_index].set(owners)
    )
    padded = jnp.concatenate([moe_input, jnp.zeros((1, feature_count), jnp.bfloat16)], axis=0)
    outgoing = padded[row_table].reshape(sources, local_count, capacity, feature_count)
    arrived = lax.all_to_all(outgoing, "seq", split_axis=0, concat_axis=0, tiled=True)
    gate_out = jnp.einsum(
        "sjnd,jdf->sjnf", arrived, gate_weight, preferred_element_type=jnp.float32
    )
    up_out = jnp.einsum("sjnd,jdf->sjnf", arrived, up_weight, preferred_element_type=jnp.float32)
    activation = (jax.nn.silu(gate_out) * up_out).astype(jnp.bfloat16)
    returned = lax.all_to_all(
        jnp.einsum(
            "sjnf,jfd->sjnd", activation, down_weight, preferred_element_type=jnp.float32
        ).astype(jnp.bfloat16),
        "seq",
        split_axis=0,
        concat_axis=0,
        tiled=True,
    )
    flat_rows = returned.reshape(expert_count * capacity, feature_count)
    picked = flat_rows[slot_index].astype(jnp.float32)
    mixture_part = jnp.sum(
        picked.reshape(row_count, top_count, feature_count) * chosen[:, :, None], axis=1
    )
    mixture = lax.psum(mixture_part.astype(jnp.bfloat16), "tensor").astype(jnp.float32)
    layer_out = (hidden + mixture).astype(jnp.bfloat16)
    key_cache = key_pages.reshape(page_rows, PAGE, span_size).astype(jnp.bfloat16)
    value_cache = value_pages.reshape(page_rows, PAGE, span_size).astype(jnp.bfloat16)
    return (layer_out, key_cache, value_cache)


def solution(mesh):
    return jax.shard_map(
        local,
        mesh=mesh,
        in_specs=(
            P("seq", None),
            P(),
            P(),
            P(),
            P(None, "tensor"),
            P(None, "tensor"),
            P(None, "tensor"),
            P("tensor", None),
            P(),
            P(),
            P("seq", None),
            P("seq", None, "tensor"),
            P("seq", None, "tensor"),
            P("seq", "tensor", None),
        ),
        out_specs=(P("seq", None), P("seq", None, "tensor"), P("seq", None, "tensor")),
        check_vma=False,
    )
```

profile of v0, /device:TPU:2, one launch (start us, length us, event | category | flops | bytes accessed | tf_op | source)
XLA Modules:
  0.0 651.1 jit_solution(417091453030510193)
XLA Ops:
  18.5 18.0 %reduce-window.20 = s32[64,8,128]{2,1,0:T(8,128)S(1)} reduce-window(s32[64,8,128]{2,1,0:T(8,128)S(1)} %fusion.52, s32[]{:T(128)} %constant.30.clone.1), window={size=1x1x128 pad=0_0x0_0x127_0}, to_apply=%region_9.10 | reduce-window | flops 8323072 | bytes 524292 | tf_op jit(solution)/shard_map/reduce-window.1
  37.8 35.6 %all-gather.3.cloned.1.call-done = bf16[4096,256]{0,1:T(8,128)(2,1)} async-done(((bf16[128,256]{0,1:T(8,128)(2,1)}), bf16[4096,256]{0,1:T(8,128)(2,1)}) %all-gather.3.cloned.1.call-update) | async-done | bytes 2097168 | tf_op jit(solution)/shard_map/all_gather | solution.py:97
  73.4 2.9 select_reduce_fusion
  79.3 49.4 %all-gather.5.cloned.1.call-done = bf16[4096,256]{1,0:T(8,128)(2,1)} async-done(((bf16[128,256]{1,0:T(8,128)(2,1)}), bf16[4096,256]{1,0:T(8,128)(2,1)}) %all-gather.5.cloned.1.call-update) | async-done | bytes 2097168 | tf_op jit(solution)/shard_map/all_gather | solution.py:98
  128.7 4.1 copy.95
  132.8 3.9 fusion.31
  137.9 4.3 scatter_custom_fusion
  142.3 74.3 %all-reduce.4.cloned.1.call-done = bf16[128,2048]{1,0:T(8,128)(2,1)} async-done(((bf16[128,2048]{1,0:T(8,128)(2,1)}), bf16[128,2048]{1,0:T(8,128)(2,1)}) %all-reduce.4.cloned.1.call-update) | async-done | bytes 524304 | tf_op jit(solution)/shard_map/psum | solution.py:144
  220.0 7.1 %gather_fusion = bf16[1536,2048]{1,0:T(8,128)(2,1)} fusion(bf16[129,2048]{1,0:T(8,128)(2,1)S(1)} %concatenate.13, s32[2048]{0:T(1024)S(1)} %pad_clamp_fusion), kind=kCustom, calls=%fused_computation | custom fusion | bytes 12589056 | tf_op jit(solution)/shard_map/gather | solution.py:172
  227.1 149.0 %all_to_all.10 = bf16[32,2,24,2048]{3,2,1,0:T(8,128)(2,1)S(1)} all-to-all(bf16[32,2,24,2048]{3,2,1,0:T(8,128)(2,1)} %bitcast.85), channel_id=1, replica_groups=mesh['seq'=32,'tensor'=8] {'seq'}, dimensions={0} | all-to-all | bytes 12582912 | tf_op jit(solution)/shard_map/all_to_all | solution.py:173
  376.1 2.7 copy-done.5
  380.7 8.9 %convert_bitcast_fusion = bf16[32,2,24,2048]{3,2,0,1:T(8,128)(2,1)} fusion(bf16[2,128,2048]{2,1,0:T(8,128)(2,1)S(1)} %copy-done, bf16[32,2,24,2048]{3,2,1,0:T(8,128)(2,1)} %copy-done.5, bf16[2,2048,128]{2,1,0:T(8,128)(2,1)S(1)} %copy-done.14, f32[32,2,24,128]{3,2,0,1:T(8,128)S(1)} %fusion.13), kind=kOutput, calls=%fused_computation.5 | convolution fusion | flops 1614938112 | bytes 15466496 | tf_op jit(solution)/shard_map/sjnf,jfd->sjnd/dot_general | solution.py:180
  389.6 6.6 %copy.84 = bf16[32,2,24,2048]{3,2,1,0:T(8,128)(2,1)} copy(bf16[32,2,24,2048]{3,2,0,1:T(8,128)(2,1)} %convert_bitcast_fusion) | data formatting | bytes 12582912 | tf_op jit(solution)/shard_map/convert_element_type | solution.py:182
  396.2 6.6 %all-to-all-start.1 = ((bf16[32,2,24,2048]{3,2,1,0:T(8,128)(2,1)}), bf16[32,2,24,2048]{3,2,1,0:T(8,128)(2,1)}, u32[]{:S(2)}, u32[]{:S(2)}) async-start(bf16[32,2,24,2048]{3,2,1,0:T(8,128)(2,1)} %copy.84), calls=%async_computation.1 | async-start | bytes 12582912 | tf_op jit(solution)/shard_map/all_to_all | solution.py:179
  403.1 3.3 copy.86
  406.4 2.4 reshape.277
  408.8 4.1 copy.87
  413.4 130.8 %all-to-all-done.1 = bf16[32,2,24,2048]{3,2,1,0:T(8,128)(2,1)} async-done(((bf16[32,2,24,2048]{3,2,1,0:T(8,128)(2,1)}), bf16[32,2,24,2048]{3,2,1,0:T(8,128)(2,1)}, u32[]{:S(2)}, u32[]{:S(2)}) %all-to-all-start.1) | async-done | bytes 6291488 | tf_op jit(solution)/shard_map/all_to_all | solution.py:179
  544.2 12.4 %gather_fusion.1 = bf16[1024,2048]{1,0:T(8,128)(2,1)} fusion(bf16[1536,2048]{1,0:T(8,128)(2,1)} %bitcast.22, s32[1024]{0:T(1024)S(1)} %broadcast_clamp_fusion), kind=kCustom, calls=%fused_computation.1 | custom fusion | bytes 8392704 | tf_op jit(solution)/shard_map/gather | solution.py:189
  556.6 7.5 %fusion = bf16[128,2048]{1,0:T(8,128)(2,1)} fusion(bf16[1024,2048]{1,0:T(8,128)(2,1)} %gather_fusion.1, f32[128,8]{1,0:T(8,128)S(1)} %copy.85), kind=kLoop, calls=%fused_computation.4 | loop fusion | flops 6029312 | bytes 4722688 | tf_op jit(solution)/shard_map/reduce_sum | solution.py:190
  567.0 2.4 reshape.278
  569.4 3.4 copy.88
  574.0 68.2 %all-reduce.6.cloned.1.call-done = bf16[128,2048]{1,0:T(8,128)(2,1)} async-done(((bf16[128,2048]{1,0:T(8,128)(2,1)}), bf16[128,2048]{1,0:T(8,128)(2,1)}) %all-reduce.6.cloned.1.call-update) | async-done | bytes 524304 | tf_op jit(solution)/shard_map/psum | solution.py:193
  642.2 2.4 add_convert_fusion
  (100 shorter events, 26.8 us)
Async XLA Ops:
  7.2 373.5 %copy-start = (bf16[2,128,2048]{2,1,0:T(8,128)(2,1)S(1)}, bf16[2,128,2048]{2,1,0:T(8,128)(2,1)}, u32[]{:S(2)}) copy-start(bf16[2,128,2048]{2,1,0:T(8,128)(2,1)} %param.27) | copy-start | bytes 3145732
  7.2 8.5 %copy-start.4 = (bf16[128,2048]{1,0:T(8,128)(2,1)S(1)}, bf16[128,2048]{1,0:T(8,128)(2,1)}, u32[]{:S(2)}) copy-start(bf16[128,2048]{1,0:T(8,128)(2,1)} %param.14) | copy-start | bytes 1572868
  7.2 8.5 %copy-start.15 = (f32[2048]{0:T(1024)S(1)}, f32[2048]{0:T(1024)}, u32[]{:S(2)}) copy-start(f32[2048]{0:T(1024)} %param.17) | copy-start | bytes 24580
  7.2 66.1 %all-gather.3.cloned.1.call-start = ((), (), s32[]{:S(2)}) async-start(), calls=%async_computation.2 | async-start | bytes 2162688 | tf_op jit(solution)/shard_map/all_gather | solution.py:97
  10.3 7.7 %copy-start.10 = (s32[128,8]{0,1:T(8,128)S(1)}, s32[128,8]{0,1:T(8,128)}, u32[]{:S(2)}) copy-start(s32[128,8]{0,1:T(8,128)} %param.24) | copy-start | bytes 12292
  15.6 113.1 %all-gather.5.cloned.1.call-start = ((), (), s32[]{:S(2)}) async-start(), calls=%async_computation.3 | async-start | bytes 2162688 | tf_op jit(solution)/shard_map/all_gather | solution.py:98
  17.9 198.7 %all-reduce.4.cloned.1.call-start = ((), (), s32[]{:S(2)}) async-start(), calls=%async_computation.4 | async-start | bytes 1048576 | tf_op jit(solution)/shard_map/psum | solution.py:144
  76.3 1.9 copy-start.2
  132.8 4.0 copy-start.8
  132.8 85.1 %copy-start.11 = (f32[2048]{0:T(1024)S(1)}, f32[2048]{0:T(1024)}, u32[]{:S(2)}) copy-start(f32[2048]{0:T(1024)} %param.22) | copy-start | bytes 24580
  219.2 0.8 copy-start.6
  227.1 151.7 %copy-start.13 = (bf16[2,2048,128]{2,1,0:T(8,128)(2,1)S(1)}, bf16[2,2048,128]{2,1,0:T(8,128)(2,1)}, u32[]{:S(2)}) copy-start(bf16[2,2048,128]{2,1,0:T(8,128)(2,1)} %param.25) | copy-start | bytes 3145732
  376.1 2.7 copy-start.5
  378.8 1.9 copy-start.14
  396.2 148.0 %all-to-all-start.1 = ((bf16[32,2,24,2048]{3,2,1,0:T(8,128)(2,1)}), bf16[32,2,24,2048]{3,2,1,0:T(8,128)(2,1)}, u32[]{:S(2)}, u32[]{:S(2)}) async-start(bf16[32,2,24,2048]{3,2,1,0:T(8,128)(2,1)} %copy.84), calls=%async_computation.1 | async-start | bytes 12582912 | tf_op jit(solution)/shard_map/all_to_all | solution.py:179
  402.8 239.4 %all-reduce.6.cloned.1.call-start = ((), (), s32[]{:S(2)}) async-start(), calls=%async_computation.5 | async-start | bytes 1048576 | tf_op jit(solution)/shard_map/psum | solution.py:193
  406.3 6.5 copy-start.7
  406.4 6.5 copy-start.9
  556.6 7.5 %copy-start.12 = (s32[256]{0:T(256)S(1)}, s32[256]{0:T(256)}, u32[]{:S(2)}) copy-start(s32[256]{0:T(256)} %param.16) | copy-start | bytes 3076
  556.6 10.4 %copy-start.3 = (bf16[4096,256]{1,0:T(8,128)(2,1)S(1)}, bf16[4096,256]{1,0:T(8,128)(2,1)}, u32[]{:S(2)}) copy-start(bf16[4096,256]{1,0:T(8,128)(2,1)} %all-gather.5.cloned.1.call-done) | copy-start | bytes 6291460
  569.3 75.2 %copy-start.1 = (bf16[2,128,2048]{2,1,0:T(8,128)(2,1)S(1)}, bf16[2,128,2048]{2,1,0:T(8,128)(2,1)}, u32[]{:S(2)}) copy-start(bf16[2,128,2048]{2,1,0:T(8,128)(2,1)} %param.27) | copy-start | bytes 3145732
Sparse Core Ops, SparseCore 0:
  15.7 57.5 all-gather.2
  76.5 52.1 all-gather.4
  138.0 78.5 all-reduce.3
  564.2 77.9 all-reduce.5
where the time goes:
time: 652 us; the launch traced here: 651 us
  waiting for transfers between devices  358 us (55%)
  blocking collectives  149 us (23%)
  local copies, waits for them, and re-layouts  58.9 us (9%)
  other arithmetic  36 us (6%)
  matrix products  27.7 us (4%)
  between operations  14.2 us (2%)
  starting transfers between devices  6.95 us (1%)
    all_to_all x1, blocking collectives, local(): lax.all_to_all(outgoing, 'seq', split_axis=0, concat_axis=0, tiled=True)  149 us
    all_to_all x1, waiting for transfers between devices, local(): lax.all_to_all(jnp.einsum('sjnf,jfd->sjnd', activation, down_weight, pref...  131 us
    psum x1, waiting for transfers between devices, local(): lax.psum(head_part.astype(jnp.bfloat16), 'tensor').astype(jnp.float32)  74.3 us
    psum x1, waiting for transfers between devices, local(): lax.psum(mixture_part.astype(jnp.bfloat16), 'tensor').astype(jnp.float32)  68.2 us
    all_gather x1, waiting for transfers between devices, local(): value_piece = lax.all_gather(value_rows, 'seq', axis=0, tiled=True)  49.4 us
    all_gather x1, waiting for transfers between devices, local(): key_piece = lax.all_gather(key_rows, 'seq', axis=0, tiled=True)  35.6 us
    another operation x5, other arithmetic  19.2 us
  transfers between devices with their start and end apart: 5, of which 5 were waited for; matrix products, arithmetic and copies ran while one was open for 8% of the time, Pallas kernels for 0%

commit v1 on v0

--- a/solution.py
+++ b/solution.py
@@ -95,7 +95,9 @@
         jnp.zeros((head_count, row_count, HEAD_DIM), jnp.float32),
     )
     key_piece = lax.all_gather(key_rows, "seq", axis=0, tiled=True)
-    value_piece = lax.all_gather(value_rows, "seq", axis=0, tiled=True)
+    value_piece = jnp.concatenate(
+        lax.all_to_all(jnp.stack([value_rows] * lax.axis_size("seq")), "seq", 0, 0), axis=0
+    )
     piece_rows = key_piece.shape[0]
     key_pages = jnp.dot(
         owned,

time: 652 us -> 624 us (0.957)
  waiting for transfers between devices: 358 us -> 298 us
  other arithmetic: 36 us -> 53.5 us
  starting transfers between devices: 6.95 us -> 18.7 us
    all_gather x1 -> x0, waiting for transfers between devices: 49.4 us -> none  [local(): value_piece = lax.all_gather(value_rows, 'seq', axis=0, tiled=True)]
    another operation x5, other arithmetic: 19.2 us -> 33.8 us
    all_gather x1, waiting for transfers between devices: 35.6 us -> 21 us  [local(): key_piece = lax.all_gather(key_rows, 'seq', axis=0, tiled=True)]
    all_to_all x0 -> x1, starting transfers between devices: none -> 11.6 us  [local(): lax.all_to_all(jnp.stack([value_rows] * lax.axis_size('seq')), 'seq', 0, 0)]
    another operation x2 -> x5, local copies, waits for them, and re-layouts: 0.09 us -> 8.15 us  [the longest x1 2.37 us: local(): value_piece.reshape(piece_rows // PAGE, PAGE * span_size)]
  transfers between devices with their start and end apart: 5 -> 5, of which waited for: 5 -> 4; matrix products, arithmetic and copies ran while one was open for 8% -> 11% of each run, Pallas kernels for 0% -> 0%
where the time goes in v1:
time: 624 us; the launch traced here: 622 us
  waiting for transfers between devices  298 us (48%)
  blocking collectives  149 us (24%)
  local copies, waits for them, and re-layouts  62.9 us (10%)
  other arithmetic  53.5 us (9%)
  matrix products  24.9 us (4%)
  starting transfers between devices  18.7 us (3%)
  between operations  14.3 us (2%)
    all_to_all x1, blocking collectives, local(): lax.all_to_all(outgoing, 'seq', split_axis=0, concat_axis=0, tiled=True)  149 us
    all_to_all x1, waiting for transfers between devices, local(): lax.all_to_all(jnp.einsum('sjnf,jfd->sjnd', activation, down_weight, pref...  135 us
    psum x1, waiting for transfers between devices, local(): lax.psum(head_part.astype(jnp.bfloat16), 'tensor').astype(jnp.float32)  75.8 us
    psum x1, waiting for transfers between devices, local(): lax.psum(mixture_part.astype(jnp.bfloat16), 'tensor').astype(jnp.float32)  66.6 us
    another operation x5, other arithmetic  33.8 us
    all_gather x1, waiting for transfers between devices, local(): key_piece = lax.all_gather(key_rows, 'seq', axis=0, tiled=True)  21 us
  transfers between devices with their start and end apart: 5, of which 4 were waited for; matrix products, arithmetic and copies ran while one was open for 11% of the time, Pallas kernels for 0%

profile of v1, /device:TPU:2, one launch (start us, length us, event | category | flops | bytes accessed | tf_op | source)
XLA Modules:
  0.0 621.5 jit_solution(5432631042168817216)
XLA Ops:
  18.0 11.6 %all-to-all-start = ((bf16[32,128,256]{2,1,0:T(8,128)(2,1)}), bf16[32,128,256]{2,1,0:T(8,128)(2,1)S(1)}, u32[]{:S(2)}, u32[]{:S(2)}) async-start(bf16[32,128,256]{2,1,0:T(8,128)(2,1)} %stack.2), calls=%async_computation | async-start | bytes 4194304 | tf_op jit(solution)/shard_map/all_to_all | solution.py:99
  31.5 31.1 %reduce-window.20 = s32[64,8,128]{2,1,0:T(8,128)S(1)} reduce-window(s32[64,8,128]{2,1,0:T(8,128)} %fusion.59, s32[]{:T(128)} %constant.30.clone.1), window={size=1x1x128 pad=0_0x0_0x127_0}, to_apply=%region_9.10 | reduce-window | flops 8323072 | bytes 524292 | tf_op jit(solution)/shard_map/reduce-window.1
  71.5 21.0 %all-gather.2.cloned.1.call-done = bf16[4096,256]{0,1:T(8,128)(2,1)} async-done(((bf16[128,256]{0,1:T(8,128)(2,1)}), bf16[4096,256]{0,1:T(8,128)(2,1)}) %all-gather.2.cloned.1.call-update) | async-done | bytes 2097168 | tf_op jit(solution)/shard_map/all_gather | solution.py:97
  92.5 3.0 select_reduce_fusion
  98.6 2.2 reshape.303
  100.8 4.4 fusion.36
  106.5 4.3 scatter_custom_fusion
  110.9 75.8 %all-reduce.4.cloned.1.call-done = bf16[128,2048]{1,0:T(8,128)(2,1)} async-done(((bf16[128,2048]{1,0:T(8,128)(2,1)}), bf16[128,2048]{1,0:T(8,128)(2,1)}) %all-reduce.4.cloned.1.call-update) | async-done | bytes 524304 | tf_op jit(solution)/shard_map/psum | solution.py:146
  190.4 7.1 %gather_fusion = bf16[1536,2048]{1,0:T(8,128)(2,1)} fusion(bf16[129,2048]{1,0:T(8,128)(2,1)S(1)} %concatenate.13, s32[2048]{0:T(1024)S(1)} %pad_clamp_fusion), kind=kCustom, calls=%fused_computation | custom fusion | bytes 12589056 | tf_op jit(solution)/shard_map/gather | solution.py:174
  197.5 149.0 %all_to_all.15 = bf16[32,2,24,2048]{3,2,1,0:T(8,128)(2,1)S(1)} all-to-all(bf16[32,2,24,2048]{3,2,1,0:T(8,128)(2,1)} %bitcast.83), channel_id=1, replica_groups=mesh['seq'=32,'tensor'=8] {'seq'}, dimensions={0} | all-to-all | bytes 12582912 | tf_op jit(solution)/shard_map/all_to_all | solution.py:175
  346.5 2.7 copy-done.7
  351.1 8.9 %convert_bitcast_fusion = bf16[32,2,24,2048]{3,2,0,1:T(8,128)(2,1)} fusion(bf16[2,128,2048]{2,1,0:T(8,128)(2,1)S(1)} %copy-done, bf16[32,2,24,2048]{3,2,1,0:T(8,128)(2,1)} %copy-done.7, bf16[2,2048,128]{2,1,0:T(8,128)(2,1)S(1)} %copy-done.21, f32[32,2,24,128]{3,2,0,1:T(8,128)S(1)} %fusion.14), kind=kOutput, calls=%fused_computation.5 | convolution fusion | flops 1614938112 | bytes 15466496 | tf_op jit(solution)/shard_map/sjnf,jfd->sjnd/dot_general | solution.py:182
  360.0 6.6 %copy.83 = bf16[32,2,24,2048]{3,2,1,0:T(8,128)(2,1)} copy(bf16[32,2,24,2048]{3,2,0,1:T(8,128)(2,1)} %convert_bitcast_fusion) | data formatting | bytes 12582912 | tf_op jit(solution)/shard_map/convert_element_type | solution.py:184
  366.6 6.7 %all-to-all-start.2 = ((bf16[32,2,24,2048]{3,2,1,0:T(8,128)(2,1)}), bf16[32,2,24,2048]{3,2,1,0:T(8,128)(2,1)}, u32[]{:S(2)}, u32[]{:S(2)}) async-start(bf16[32,2,24,2048]{3,2,1,0:T(8,128)(2,1)} %copy.83), calls=%async_computation.2 | async-start | bytes 12582912 | tf_op jit(solution)/shard_map/all_to_all | solution.py:181
  373.6 2.4 reshape_reshape.7
  376.0 3.3 copy.87
  379.8 134.8 %all-to-all-done.2 = bf16[32,2,24,2048]{3,2,1,0:T(8,128)(2,1)} async-done(((bf16[32,2,24,2048]{3,2,1,0:T(8,128)(2,1)}), bf16[32,2,24,2048]{3,2,1,0:T(8,128)(2,1)}, u32[]{:S(2)}, u32[]{:S(2)}) %all-to-all-start.2) | async-done | bytes 6291488 | tf_op jit(solution)/shard_map/all_to_all | solution.py:181
  514.6 12.4 %gather_fusion.1 = bf16[1024,2048]{1,0:T(8,128)(2,1)} fusion(bf16[1536,2048]{1,0:T(8,128)(2,1)} %bitcast.21, s32[1024]{0:T(1024)S(1)} %broadcast_clamp_fusion), kind=kCustom, calls=%fused_computation.1 | custom fusion | bytes 8392704 | tf_op jit(solution)/shard_map/gather | solution.py:191
  527.0 7.3 %fusion = bf16[128,2048]{1,0:T(8,128)(2,1)} fusion(bf16[1024,2048]{1,0:T(8,128)(2,1)} %gather_fusion.1, f32[128,8]{1,0:T(8,128)S(1)} %copy.84), kind=kLoop, calls=%fused_computation.4 | loop fusion | flops 6029312 | bytes 4722688 | tf_op jit(solution)/shard_map/reduce_sum | solution.py:192
  535.7 3.3 copy.85
  539.0 2.4 reshape.272
  541.3 3.4 copy.86
  546.0 66.6 %all-reduce.6.cloned.1.call-done = bf16[128,2048]{1,0:T(8,128)(2,1)} async-done(((bf16[128,2048]{1,0:T(8,128)(2,1)}), bf16[128,2048]{1,0:T(8,128)(2,1)}) %all-reduce.6.cloned.1.call-update) | async-done | bytes 524304 | tf_op jit(solution)/shard_map/psum | solution.py:195
  612.6 2.4 add_convert_fusion
  (114 shorter events, 34.6 us)
Async XLA Ops:
  7.2 343.9 %copy-start = (bf16[2,128,2048]{2,1,0:T(8,128)(2,1)S(1)}, bf16[2,128,2048]{2,1,0:T(8,128)(2,1)}, u32[]{:S(2)}) copy-start(bf16[2,128,2048]{2,1,0:T(8,128)(2,1)} %param.27) | copy-start | bytes 3145732
  7.2 8.9 %copy-start.5 = (bf16[128,2048]{1,0:T(8,128)(2,1)S(1)}, bf16[128,2048]{1,0:T(8,128)(2,1)}, u32[]{:S(2)}) copy-start(bf16[128,2048]{1,0:T(8,128)(2,1)} %param.14) | copy-start | bytes 1572868
  7.2 8.8 %copy-start.22 = (f32[2048]{0:T(1024)S(1)}, f32[2048]{0:T(1024)}, u32[]{:S(2)}) copy-start(f32[2048]{0:T(1024)} %param.17) | copy-start | bytes 24580
  7.2 8.8 %copy-start.19 = (bf16[2048,256]{1,0:T(8,128)(2,1)S(1)}, bf16[2048,256]{1,0:T(8,128)(2,1)}, u32[]{:S(2)}) copy-start(bf16[2048,256]{1,0:T(8,128)(2,1)} %param.20) | copy-start | bytes 3145732
  7.2 85.3 %all-gather.2.cloned.1.call-start = ((), (), s32[]{:S(2)}) async-start(), calls=%async_computation.3 | async-start | bytes 2162688 | tf_op jit(solution)/shard_map/all_gather | solution.py:97
  7.3 3.4 copy-start.17
  15.2 14.4 %copy-start.12 = (s32[128,8]{0,1:T(8,128)S(1)}, s32[128,8]{0,1:T(8,128)}, u32[]{:S(2)}) copy-start(s32[128,8]{0,1:T(8,128)} %param.24) | copy-start | bytes 12292
  18.0 80.6 %all-to-all-start = ((bf16[32,128,256]{2,1,0:T(8,128)(2,1)}), bf16[32,128,256]{2,1,0:T(8,128)(2,1)S(1)}, u32[]{:S(2)}, u32[]{:S(2)}) async-start(bf16[32,128,256]{2,1,0:T(8,128)(2,1)} %stack.2), calls=%async_computation | async-start | bytes 4194304 | tf_op jit(solution)/shard_map/all_to_all | solution.py:99
  29.6 157.1 %all-reduce.4.cloned.1.call-start = ((), (), s32[]{:S(2)}) async-start(), calls=%async_computation.4 | async-start | bytes 1048576 | tf_op jit(solution)/shard_map/psum | solution.py:146
  92.5 5.0 copy-start.6
  95.6 1.9 copy-start.4
  98.6 6.7 %copy-start.2 = (bf16[32,128,256]{2,1,0:T(8,128)(2,1)}, bf16[32,128,256]{2,1,0:T(8,128)(2,1)S(1)}, u32[]{:S(2)}) copy-start(bf16[32,128,256]{2,1,0:T(8,128)(2,1)S(1)} %all-to-all-done) | copy-start | bytes 6291460
  100.8 4.5 copy-start.10
  100.8 5.6 copy-start.13
  100.8 87.3 %copy-start.14 = (f32[2048]{0:T(1024)S(1)}, f32[2048]{0:T(1024)}, u32[]{:S(2)}) copy-start(f32[2048]{0:T(1024)} %param.22) | copy-start | bytes 24580
  197.5 151.7 %copy-start.20 = (bf16[2,2048,128]{2,1,0:T(8,128)(2,1)S(1)}, bf16[2,2048,128]{2,1,0:T(8,128)(2,1)}, u32[]{:S(2)}) copy-start(bf16[2,2048,128]{2,1,0:T(8,128)(2,1)} %param.25) | copy-start | bytes 3145732
  346.5 2.7 copy-start.7
  366.6 7.0 %copy-start.3 = (bf16[32,128,256]{2,1,0:T(8,128)(2,1)S(1)}, bf16[32,128,256]{2,1,0:T(8,128)(2,1)}, u32[]{:S(2)}) copy-start(bf16[32,128,256]{2,1,0:T(8,128)(2,1)} %copy-done.2) | copy-start | bytes 6291460
  366.6 148.0 %all-to-all-start.2 = ((bf16[32,2,24,2048]{3,2,1,0:T(8,128)(2,1)}), bf16[32,2,24,2048]{3,2,1,0:T(8,128)(2,1)}, u32[]{:S(2)}, u32[]{:S(2)}) async-start(bf16[32,2,24,2048]{3,2,1,0:T(8,128)(2,1)} %copy.83), calls=%async_computation.2 | async-start | bytes 12582912 | tf_op jit(solution)/shard_map/all_to_all | solution.py:181
  373.3 239.3 %all-reduce.6.cloned.1.call-start = ((), (), s32[]{:S(2)}) async-start(), calls=%async_computation.5 | async-start | bytes 1048576 | tf_op jit(solution)/shard_map/psum | solution.py:195
  373.6 5.7 copy-start.9
  373.6 5.7 copy-start.11
  527.0 7.4 %copy-start.15 = (s32[256]{0:T(256)S(1)}, s32[256]{0:T(256)}, u32[]{:S(2)}) copy-start(s32[256]{0:T(256)} %param.16) | copy-start | bytes 3076
  541.3 73.7 %copy-start.1 = (bf16[2,128,2048]{2,1,0:T(8,128)(2,1)S(1)}, bf16[2,128,2048]{2,1,0:T(8,128)(2,1)}, u32[]{:S(2)}) copy-start(bf16[2,128,2048]{2,1,0:T(8,128)(2,1)} %param.27) | copy-start | bytes 3145732
  (4 other events, 4.9 us)
Sparse Core Ops, SparseCore 0:
  16.1 76.3 all-gather.1
  106.6 80.0 all-reduce.3
  534.5 78.0 all-reduce.5
